TPU v7x, 32 devices: a whole 2x2x4 slice. The times are simulated.
32 devices in a mesh: groups: 2 (over x), win: 4 (over y, core), rcv: 4 (over z).
Axes of the slice: x: 2, y: 2, z: 4, core: 2. Of those that a mesh axis runs over, the one named last changes fastest.
Arguments:
- traces: bfloat16 [32, 768, 4096], P('win', ('groups', 'rcv')), parts along dimension 1, may hold values from -6 to 6
- valid: int32 [64], P(('groups', 'win')), parts along dimension 0, may hold values 0 or 1
- src_station: int32 [64], P('groups'), parts along dimension 0, may hold values from 0 to 383, as said below
Outputs:
- stacks: float32 [32, 768, 2, 512], P(None, ('groups', 'rcv'), None, 'win'), parts along dimension 1
There are 2 independent parts, one for each index of `groups`. A program takes and returns all parts, laid end to end along the dimension named above; each array names one. Nothing has to cross between parts.
Inputs may be any that keep to these rules, and one draw needn't show every extreme that they name: `src_station`: distinct stations; station 0 and station 384 - 1 are always among them.
All inputs are finite; a program needn't handle non-finite values. No bound on the sum of `valid` on one device may be relied on, other than what follows from the above.
Results may differ from a plain program's by a relative error of at most 0.0049.
Values may be sent and summed in bfloat16 or wider, within the bound.
A program may use at most 128 MiB of HBM per device.

v0:
```python
import math
import jax
import jax.numpy as jnp
import ml_dtypes
import numpy as np
from jax import lax
from jax.sharding import PartitionSpec as P

F = 512


def band_table(count, bins, first):
    samples = np.arange(count, dtype=np.int64)
    freqs = first + np.arange(bins, dtype=np.int64)
    phase = samples[:, None] * freqs[None, :] % count
    angle = phase.astype(np.float64) * (2.0 * math.pi / count)
    return np.concatenate([np.cos(angle), -np.sin(angle)], axis=1).astype(ml_dtypes.bfloat16)


def body(traces, valid, src_station):
    w_dev, r_dev, samples = traces.shape
    bins = F
    n_win = lax.axis_size("win")
    f_dev = bins // n_win
    table = jnp.asarray(band_table(samples, bins, samples // 16))
    spectra = jnp.dot(
        traces.reshape(w_dev * r_dev, samples), table, preferred_element_type=jnp.float32
    )
    power = jnp.sum(spectra * spectra, axis=1, keepdims=True) / bins
    keep = jnp.repeat(valid.astype(jnp.float32), r_dev)[:, None]
    white = (spectra * (lax.rsqrt(power + 1e-06) * keep)).astype(jnp.bfloat16)
    white = white.reshape(w_dev * r_dev, 2, n_win, f_dev)
    pieces = jnp.transpose(white, (2, 1, 0, 3))
    got = lax.all_to_all(pieces, "win", 0, 0, tiled=True)
    got = got.reshape(n_win, 2, w_dev, r_dev, f_dev)
    offset = lax.axis_index("rcv") * r_dev
    station_ids = offset + jnp.arange(r_dev, dtype=jnp.int32)
    selector = (src_station[:, None] == station_ids[None, :]).astype(jnp.bfloat16)
    rows = jnp.einsum("sr,gcwrf->gcwsf", selector, got, preferred_element_type=jnp.float32)
    src = lax.psum(rows.astype(jnp.bfloat16), "rcv")
    scale = 1.0 / math.sqrt(w_dev * n_win)
    turned = jnp.stack([got[:, 1], -got[:, 0]], axis=1)
    real = jnp.einsum("gcwsf,gcwrf->srf", src, got, preferred_element_type=jnp.float32)
    imag = jnp.einsum("gcwsf,gcwrf->srf", src, turned, preferred_element_type=jnp.float32)
    return jnp.stack([real, imag], axis=2) * scale


def solution(mesh):
    return jax.shard_map(
        body,
        mesh=mesh,
        in_specs=(P("win", ("groups", "rcv"), None), P(("groups", "win")), P("groups")),
        out_specs=P(None, ("groups", "rcv"), None, "win"),
        check_vma=False,
    )
```

profile of v0, /device:TPU:0, one launch (start us, length us, event | category | flops | bytes accessed | tf_op | source)
XLA Modules:
  0.0 113.4 jit_solution(5430483913655910019)
XLA Ops:
  6.5 0.7 convert_element_type.13
  7.2 0.1 broadcast_in_dim.2
  7.3 0.1 broadcast_in_dim_reshape.3
  7.3 11.0 %multiply_reduce_fusion = (f32[768]{0:T(1024)S(1)}, f32[1024,768]{1,0:T(8,128)S(1)}) fusion(bf16[4096,1024]{1,0:T(8,128)(2,1)} %constant.17.clone, bf16[768,4096]{1,0:T(8,128)(2,1)} %bitcast.42), kind=kOutput, calls=%fused_computation.2 | convolution fusion | flops 6444022784 | bytes 17828864 | tf_op jit(solution)/shard_map/dot_general | solution.py:26
  18.4 0.3 multiply_convert_fusion
  18.7 1.3 %copy.31 = bf16[768,2,4,128]{0,3,1,2:T(8,128)(2,1)} copy(bf16[768,2,4,128]{0,3,2,1:T(8,128)(2,1)S(1)} %bitcast.41) | data formatting | bytes 3145728 | tf_op jit(solution)/shard_map/reshape | solution.py:32
  19.9 4.2 %all-to-all-start = ((bf16[4,2,768,128]{2,3,1,0:T(8,128)(2,1)}), bf16[4,2,768,128]{2,3,1,0:T(8,128)(2,1)S(1)}, u32[]{:S(2)}, u32[]{:S(2)}) async-start(bf16[4,2,768,128]{2,3,1,0:T(8,128)(2,1)} %bitcast.35), calls=%async_computation | async-start | bytes 3145728 | tf_op jit(solution)/shard_map/all_to_all | solution.py:34
  24.2 0.0 copy-start.1
  24.2 0.0 all-reduce.2.cloned.1.call-start
  24.2 20.1 %all-to-all-done = bf16[4,2,768,128]{2,3,1,0:T(8,128)(2,1)S(1)} async-done(((bf16[4,2,768,128]{2,3,1,0:T(8,128)(2,1)}), bf16[4,2,768,128]{2,3,1,0:T(8,128)(2,1)S(1)}, u32[]{:S(2)}, u32[]{:S(2)}) %all-to-all-start) | async-done | bytes 1572896 | tf_op jit(solution)/shard_map/all_to_all | solution.py:34
  44.2 0.9 copy.19
  45.1 0.0 copy-done.1
  45.2 1.2 %fusion = bf16[4,2,8,32,128]{4,3,2,1,0:T(8,128)(2,1)} fusion(bf16[4,2,8,96,128]{4,3,2,1,0:T(8,128)(2,1)S(1)} %bitcast.36, s32[96]{0:T(128)S(1)} %iota_add_fusion, s32[32]{0:T(128)S(1)} %copy-done.1), kind=kOutput, calls=%fused_computation.8 | convolution fusion | flops 50596864 | bytes 2097664 | tf_op jit(solution)/shard_map/sr,gcwrf->gcwsf/dot_general | solution.py:39
  46.4 0.0 all-reduce.2.cloned.1.call-update
  46.4 3.0 %copy.20 = bf16[4,2,8,96,128]{3,2,0,1,4:T(8,128)(2,1)} copy(bf16[4,2,8,96,128]{4,3,2,1,0:T(8,128)(2,1)S(1)} %bitcast.37) | data formatting | bytes 3145728 | tf_op jit(solution)/shard_map/reshape | solution.py:35
  49.4 0.2 fusion.5
  49.5 0.1 pad_maximum_fusion
  49.7 2.9 %copy.23 = bf16[4,2,8,96,128]{3,2,0,1,4:T(8,128)(2,1)} copy(bf16[4,2,8,96,128]{4,3,2,1,0:T(8,128)(2,1)S(1)} %pad_maximum_fusion) | data formatting | bytes 3145728 | tf_op jit(solution)/shard_map/stack | solution.py:42
  52.6 33.3 %all-reduce.2.cloned.1.call-done = bf16[4,2,8,32,128]{4,3,2,1,0:T(8,128)(2,1)} async-done(((bf16[4,2,8,32,128]{4,3,2,1,0:T(8,128)(2,1)}), bf16[4,2,8,32,128]{4,3,2,1,0:T(8,128)(2,1)}) %all-reduce.2.cloned.1.call-update) | async-done | bytes 524304 | tf_op jit(solution)/shard_map/psum | solution.py:40
  85.8 3.9 %copy.21 = bf16[4,2,8,32,128]{3,2,0,1,4:T(8,128)(2,1)S(1)} copy(bf16[4,2,8,32,128]{4,3,2,1,0:T(8,128)(2,1)} %all-reduce.2.cloned.1.call-done) | data formatting | bytes 1048576 | tf_op jit(solution)/shard_map/psum | solution.py:40
  89.7 3.6 %convolution_bitcast_fusion = f32[128,96,32]{1,2,0:T(8,128)} fusion(bf16[4,2,8,96,128]{3,2,0,1,4:T(8,128)(2,1)} %copy.23, bf16[4,2,8,32,128]{3,2,0,1,4:T(8,128)(2,1)S(1)} %copy.21), kind=kOutput, calls=%fused_computation.3 | convolution fusion | flops 50331648 | bytes 3670016 | tf_op jit(solution)/shard_map/gcwsf,gcwrf->srf/dot_general | solution.py:44
  93.4 2.9 %copy.25 = f32[128,96,32]{0,1,2:T(8,128)} copy(f32[128,96,32]{1,2,0:T(8,128)} %convolution_bitcast_fusion) | data formatting | bytes 3145728 | tf_op jit(solution)/shard_map/gcwsf,gcwrf->srf/dot_general | solution.py:44
  96.3 3.6 %convolution_bitcast_fusion.1 = f32[128,96,32]{1,2,0:T(8,128)} fusion(bf16[4,2,8,96,128]{3,2,0,1,4:T(8,128)(2,1)} %copy.20, bf16[4,2,8,32,128]{3,2,0,1,4:T(8,128)(2,1)S(1)} %copy.21), kind=kOutput, calls=%fused_computation.4 | convolution fusion | flops 50331648 | bytes 3670016 | tf_op jit(solution)/shard_map/gcwsf,gcwrf->srf/dot_general | solution.py:43
  100.0 0.0 copy-start
  100.0 2.2 %copy.22 = f32[128,96,32]{0,1,2:T(8,128)S(1)} copy(f32[128,96,32]{1,2,0:T(8,128)} %convolution_bitcast_fusion.1) | data formatting | bytes 3145728 | tf_op jit(solution)/shard_map/gcwsf,gcwrf->srf/dot_general | solution.py:43
  102.1 0.0 copy-done
  102.1 0.3 maximum_multiply_fusion
  102.5 4.1 %copy.26 = f32[32,96,2,128]{3,2,1,0:T(2,128)} copy(f32[32,96,2,128]{3,1,2,0:T(8,128)S(1)} %maximum_multiply_fusion) | data formatting | bytes 6291456 | tf_op jit(solution)/shard_map/mul | solution.py:45
  (2 shorter events, 0.0 us)
Async XLA Ops:
  19.9 24.3 %all-to-all-start = ((bf16[4,2,768,128]{2,3,1,0:T(8,128)(2,1)}), bf16[4,2,768,128]{2,3,1,0:T(8,128)(2,1)S(1)}, u32[]{:S(2)}, u32[]{:S(2)}) async-start(bf16[4,2,768,128]{2,3,1,0:T(8,128)(2,1)} %bitcast.35), calls=%async_computation | async-start | bytes 3145728 | tf_op jit(solution)/shard_map/all_to_all | solution.py:34
  24.2 21.0 %copy-start.1 = (s32[32]{0:T(128)S(1)}, s32[32]{0:T(128)}, u32[]{:S(2)}) copy-start(s32[32]{0:T(128)} %param.6) | copy-start | bytes 388
  24.2 61.7 %all-reduce.2.cloned.1.call-start = ((), (), s32[]{:S(2)}) async-start(), calls=%async_computation.1 | async-start | bytes 1048576 | tf_op jit(solution)/shard_map/psum | solution.py:40
  100.0 2.2 %copy-start = (f32[128,96,32]{0,1,2:T(8,128)S(1)}, f32[128,96,32]{0,1,2:T(8,128)}, u32[]{:S(2)}) copy-start(f32[128,96,32]{0,1,2:T(8,128)} %copy.25) | copy-start | bytes 4718596
Sparse Core Ops, SparseCore 0:
  46.5 39.2 all-reduce.1
where the time goes:
time: 114 us; the launch traced here: 113 us
  waiting for transfers between devices  53.4 us (47%)
  local copies, waits for them, and re-layouts  21.2 us (19%)
  matrix products  19.5 us (17%)
  between operations  13.5 us (12%)
  starting transfers between devices  4.24 us (4%)
  other arithmetic  1.54 us (1%)
    psum x1, waiting for transfers between devices, body(): src = lax.psum(rows.astype(jnp.bfloat16), 'rcv')  33.3 us
    all_to_all x1, waiting for transfers between devices, body(): got = lax.all_to_all(pieces, 'win', 0, 0, tiled=True)  20.1 us
    dot_general x1, matrix products, body(): jnp.dot(traces.reshape(w_dev * r_dev, samples), table, preferred_element_...  11 us
    all_to_all x1, starting transfers between devices, body(): got = lax.all_to_all(pieces, 'win', 0, 0, tiled=True)  4.24 us
    mul x1, local copies, waits for them, and re-layouts, body(): return jnp.stack([real, imag], axis=2) * scale  4.1 us
    psum x1, local copies, waits for them, and re-layouts, body(): src = lax.psum(rows.astype(jnp.bfloat16), 'rcv')  3.88 us
    dot_general x1, matrix products, body(): jnp.einsum('gcwsf,gcwrf->srf', src, got, preferred_element_type=jnp.float32)  3.65 us
    dot_general x1, matrix products, body(): jnp.einsum('gcwsf,gcwrf->srf', src, turned, preferred_element_type=jnp.fl...  3.64 us
  transfers between devices with their start and end apart: 2, of which 2 were waited for; matrix products, arithmetic and copies ran while one was open for 5% of the time, Pallas kernels for 0%

commit v1 on v0

--- a/solution.py
+++ b/solution.py
@@ -37,7 +37,7 @@
     station_ids = offset + jnp.arange(r_dev, dtype=jnp.int32)
     selector = (src_station[:, None] == station_ids[None, :]).astype(jnp.bfloat16)
     rows = jnp.einsum("sr,gcwrf->gcwsf", selector, got, preferred_element_type=jnp.float32)
-    src = lax.psum(rows.astype(jnp.bfloat16), "rcv")
+    src = jnp.sum(lax.all_gather(rows.astype(jnp.bfloat16), "rcv"), axis=0)
     scale = 1.0 / math.sqrt(w_dev * n_win)
     turned = jnp.stack([got[:, 1], -got[:, 0]], axis=1)
     real = jnp.einsum("gcwsf,gcwrf->srf", src, got, preferred_element_type=jnp.float32)

time: 114 us -> 122 us (1.070)
  waiting for transfers between devices: 53.4 us -> 61 us
  other arithmetic: 1.54 us -> 3.51 us
    all_gather x0 -> x1, waiting for transfers between devices: none -> 41 us  [body(): src = jnp.sum(lax.all_gather(rows.astype(jnp.bfloat16), 'rcv'), axis=0)]
    psum x1 -> x0, waiting for transfers between devices: 33.3 us -> none  [body(): src = lax.psum(rows.astype(jnp.bfloat16), 'rcv')]
    psum x1 -> x0, local copies, waits for them, and re-layouts: 3.88 us -> none  [body(): src = lax.psum(rows.astype(jnp.bfloat16), 'rcv')]
    reduce_sum x0 -> x1, local copies, waits for them, and re-layouts: none -> 2.98 us  [body(): src = jnp.sum(lax.all_gather(rows.astype(jnp.bfloat16), 'rcv'), axis=0)]
    reduce_sum x0 -> x1, other arithmetic: none -> 1.97 us  [body(): src = jnp.sum(lax.all_gather(rows.astype(jnp.bfloat16), 'rcv'), axis=0)]
where the time goes in v1:
time: 122 us
  waiting for transfers between devices  61 us (50%)
  local copies, waits for them, and re-layouts  20.3 us (17%)
  matrix products  19.5 us (16%)
  between operations  13.5 us (11%)
  starting transfers between devices  4.24 us (3%)
  other arithmetic  3.51 us (3%)
    all_gather x1, waiting for transfers between devices, body(): src = jnp.sum(lax.all_gather(rows.astype(jnp.bfloat16), 'rcv'), axis=0)  41 us
    all_to_all x1, waiting for transfers between devices, body(): got = lax.all_to_all(pieces, 'win', 0, 0, tiled=True)  20.1 us
    dot_general x1, matrix products, body(): jnp.dot(traces.reshape(w_dev * r_dev, samples), table, preferred_element_...  11 us
    all_to_all x1, starting transfers between devices, body(): got = lax.all_to_all(pieces, 'win', 0, 0, tiled=True)  4.24 us
    mul x1, local copies, waits for them, and re-layouts, body(): return jnp.stack([real, imag], axis=2) * scale  4.1 us
    dot_general x1, matrix products, body(): jnp.einsum('gcwsf,gcwrf->srf', src, got, preferred_element_type=jnp.float32)  3.65 us
    dot_general x1, matrix products, body(): jnp.einsum('gcwsf,gcwrf->srf', src, turned, preferred_element_type=jnp.fl...  3.64 us
    reduce_sum x1, local copies, waits for them, and re-layouts, body(): src = jnp.sum(lax.all_gather(rows.astype(jnp.bfloat16), 'rcv'), axis=0)  2.98 us
  transfers between devices with their start and end apart: 2, of which 2 were waited for; matrix products, arithmetic and copies ran while one was open for 5% of the time, Pallas kernels for 0%

profile of v1, /device:TPU:0, one launch (start us, length us, event | category | flops | bytes accessed | tf_op | source)
XLA Modules:
  0.0 122.2 jit_solution(1658166313044403842)
XLA Ops:
  6.5 0.7 convert_element_type.15
  7.2 0.1 broadcast_in_dim.2
  7.3 0.1 broadcast_in_dim_reshape.3
  7.3 11.0 %multiply_reduce_fusion = (f32[768]{0:T(1024)S(1)}, f32[1024,768]{1,0:T(8,128)S(1)}) fusion(bf16[4096,1024]{1,0:T(8,128)(2,1)} %constant.19.clone, bf16[768,4096]{1,0:T(8,128)(2,1)} %bitcast.44), kind=kOutput, calls=%fused_computation.2 | convolution fusion | flops 6444022784 | bytes 17828864 | tf_op jit(solution)/shard_map/dot_general | solution.py:26
  18.4 0.3 multiply_convert_fusion
  18.7 1.3 %copy.29 = bf16[768,2,4,128]{0,3,1,2:T(8,128)(2,1)} copy(bf16[768,2,4,128]{0,3,2,1:T(8,128)(2,1)S(1)} %bitcast.42) | data formatting | bytes 3145728 | tf_op jit(solution)/shard_map/reshape | solution.py:32
  19.9 4.2 %all-to-all-start = ((bf16[4,2,768,128]{2,3,1,0:T(8,128)(2,1)}), bf16[4,2,768,128]{2,3,1,0:T(8,128)(2,1)S(1)}, u32[]{:S(2)}, u32[]{:S(2)}) async-start(bf16[4,2,768,128]{2,3,1,0:T(8,128)(2,1)} %bitcast.36), calls=%async_computation | async-start | bytes 3145728 | tf_op jit(solution)/shard_map/all_to_all | solution.py:34
  24.2 0.0 copy-start.1
  24.2 0.0 all-gather.3.cloned.1.call-start
  24.2 20.1 %all-to-all-done = bf16[4,2,768,128]{2,3,1,0:T(8,128)(2,1)S(1)} async-done(((bf16[4,2,768,128]{2,3,1,0:T(8,128)(2,1)}), bf16[4,2,768,128]{2,3,1,0:T(8,128)(2,1)S(1)}, u32[]{:S(2)}, u32[]{:S(2)}) %all-to-all-start) | async-done | bytes 1572896 | tf_op jit(solution)/shard_map/all_to_all | solution.py:34
  44.2 0.9 copy.17
  45.1 0.0 copy-done.1
  45.2 1.2 fusion
  46.4 0.0 all-gather.3.cloned.1.call-update
  46.4 3.0 %copy.18 = bf16[4,2,8,96,128]{3,2,0,1,4:T(8,128)(2,1)} copy(bf16[4,2,8,96,128]{4,3,2,1,0:T(8,128)(2,1)S(1)} %bitcast.38) | data formatting | bytes 3145728 | tf_op jit(solution)/shard_map/reshape | solution.py:35
  49.4 0.2 fusion.5
  49.5 0.1 pad_maximum_fusion
  49.7 2.9 %copy.21 = bf16[4,2,8,96,128]{3,2,0,1,4:T(8,128)(2,1)} copy(bf16[4,2,8,96,128]{4,3,2,1,0:T(8,128)(2,1)S(1)} %pad_maximum_fusion) | data formatting | bytes 3145728 | tf_op jit(solution)/shard_map/stack | solution.py:42
  52.5 41.0 %all-gather.3.cloned.1.call-done = bf16[16,2,8,32,128]{4,3,2,1,0:T(8,128)(2,1)} async-done(((bf16[4,2,8,32,128]{4,3,2,1,0:T(8,128)(2,1)}), bf16[16,2,8,32,128]{4,3,2,1,0:T(8,128)(2,1)}) %all-gather.3.cloned.1.call-update) | async-done | bytes 2097168 | tf_op jit(solution)/shard_map/all_gather | solution.py:40
  93.5 2.0 %reduce_sum.22 = bf16[4,2,8,32,128]{4,3,2,1,0:T(8,128)(2,1)S(1)} reduce(bf16[4,4,2,8,32,128]{5,4,3,2,1,0:T(8,128)(2,1)} %bitcast.43, bf16[]{:T(256)} %constant.17.clone.1), dimensions={0}, to_apply=%region_1.0 | reduce | flops 786432 | bytes 2621442 | tf_op jit(solution)/shard_map/reduce_sum | solution.py:40
  95.5 3.0 %copy.19 = bf16[4,2,8,32,128]{3,2,0,1,4:T(8,128)(2,1)S(1)} copy(bf16[4,2,8,32,128]{4,3,2,1,0:T(8,128)(2,1)S(1)} %reduce_sum.22) | data formatting | bytes 1048576 | tf_op jit(solution)/shard_map/reduce_sum | solution.py:40
  98.5 3.6 %convolution_bitcast_fusion = f32[128,96,32]{1,2,0:T(8,128)} fusion(bf16[4,2,8,96,128]{3,2,0,1,4:T(8,128)(2,1)} %copy.21, bf16[4,2,8,32,128]{3,2,0,1,4:T(8,128)(2,1)S(1)} %copy.19), kind=kOutput, calls=%fused_computation.3 | convolution fusion | flops 50331648 | bytes 3670016 | tf_op jit(solution)/shard_map/gcwsf,gcwrf->srf/dot_general | solution.py:44
  102.1 2.9 %copy.23 = f32[128,96,32]{0,1,2:T(8,128)} copy(f32[128,96,32]{1,2,0:T(8,128)} %convolution_bitcast_fusion) | data formatting | bytes 3145728 | tf_op jit(solution)/shard_map/gcwsf,gcwrf->srf/dot_general | solution.py:44
  105.0 3.6 %convolution_bitcast_fusion.1 = f32[128,96,32]{1,2,0:T(8,128)} fusion(bf16[4,2,8,96,128]{3,2,0,1,4:T(8,128)(2,1)} %copy.18, bf16[4,2,8,32,128]{3,2,0,1,4:T(8,128)(2,1)S(1)} %copy.19), kind=kOutput, calls=%fused_computation.4 | convolution fusion | flops 50331648 | bytes 3670016 | tf_op jit(solution)/shard_map/gcwsf,gcwrf->srf/dot_general | solution.py:43
  108.7 0.0 copy-start
  108.7 2.2 %copy.20 = f32[128,96,32]{0,1,2:T(8,128)S(1)} copy(f32[128,96,32]{1,2,0:T(8,128)} %convolution_bitcast_fusion.1) | data formatting | bytes 3145728 | tf_op jit(solution)/shard_map/gcwsf,gcwrf->srf/dot_general | solution.py:43
  110.9 0.0 copy-done
  110.9 0.3 maximum_multiply_fusion
  111.2 4.1 %copy.24 = f32[32,96,2,128]{3,2,1,0:T(2,128)} copy(f32[32,96,2,128]{3,1,2,0:T(8,128)S(1)} %maximum_multiply_fusion) | data formatting | bytes 6291456 | tf_op jit(solution)/shard_map/mul | solution.py:45
  (2 shorter events, 0.0 us)
Async XLA Ops:
  19.9 24.3 %all-to-all-start = ((bf16[4,2,768,128]{2,3,1,0:T(8,128)(2,1)}), bf16[4,2,768,128]{2,3,1,0:T(8,128)(2,1)S(1)}, u32[]{:S(2)}, u32[]{:S(2)}) async-start(bf16[4,2,768,128]{2,3,1,0:T(8,128)(2,1)} %bitcast.36), calls=%async_computation | async-start | bytes 3145728 | tf_op jit(solution)/shard_map/all_to_all | solution.py:34
  24.2 21.0 %copy-start.1 = (s32[32]{0:T(128)S(1)}, s32[32]{0:T(128)}, u32[]{:S(2)}) copy-start(s32[32]{0:T(128)} %param.6) | copy-start | bytes 388
  24.2 69.3 %all-gather.3.cloned.1.call-start = ((), (), s32[]{:S(2)}) async-start(), calls=%async_computation.1 | async-start | bytes 2621440 | tf_op jit(solution)/shard_map/all_gather | solution.py:40
  108.7 2.2 %copy-start = (f32[128,96,32]{0,1,2:T(8,128)S(1)}, f32[128,96,32]{0,1,2:T(8,128)}, u32[]{:S(2)}) copy-start(f32[128,96,32]{0,1,2:T(8,128)} %copy.23) | copy-start | bytes 4718596
Sparse Core Ops, SparseCore 0:
  46.5 46.9 all-gather.2
